TPU v7x, 32 devices: a whole 2x2x4 slice. The times are simulated.
32 devices in a mesh: sta: 16 (over z, x, core), tm: 2 (over y).
Axes of the slice: x: 2, y: 2, z: 4, core: 2. Of those that a mesh axis runs over, the one named last changes fastest.
Arguments:
- spectra: float32 [2, 64, 512, 256], P(None, 'tm', 'sta'), may hold values from -6 to 6
- valid: int32 [64, 512], P('tm', 'sta'), may hold values 0 or 1
Outputs:
- stacks: float32 [2, 4, 512, 32, 256], P(None, None, 'sta', 'tm')
All inputs are finite; a program needn't handle non-finite values. No bound on the sum of `valid` on one device may be relied on, other than what follows from the above.
Results may differ from a plain program's by a relative error of at most 0.0001.
Values sent between devices are 32-bit elements; how exact they have to be, the bound alone decides.
A program may use at most 192 MiB of HBM per device.

v0:
```python
import functools

import jax
import jax.numpy as jnp
from jax import lax
from jax.experimental import pallas as pl
from jax.experimental.pallas import tpu as pltpu
from jax.sharding import PartitionSpec as P

OFFSETS = 4
LANES = 128
ROWS = 4


def passed_along(value, axis, steps):
    count = lax.axis_size(axis)
    pairs = [(source, (source + steps) % count) for source in range(count)]
    return lax.ppermute(value, axis, pairs)


def whiten_local(spectra, valid):
    power = jnp.mean(spectra[0] * spectra[0] + spectra[1] * spectra[1], axis=-1, keepdims=True)
    scale = valid.astype(jnp.float32)[..., None] / jnp.sqrt(power + 1e-06)
    return spectra * scale[None]


def by_bins(whitened):
    chans, wins, stats, bins = whitened.shape
    return jnp.transpose(whitened, (3, 0, 1, 2)).reshape(bins, chans * wins, stats)


def cross_block(own, flipped, other, windows):
    real_part = jnp.einsum("fka,fkb->fab", own, other, precision=lax.Precision.HIGHEST)
    imag_part = jnp.einsum("fka,fkb->fab", flipped, other, precision=lax.Precision.HIGHEST)
    both = jnp.stack((real_part, imag_part)) / windows
    return jnp.transpose(both, (0, 2, 3, 1))


def on_device_general(spectra, valid):
    whitened = whiten_local(spectra, valid)
    windows = spectra.shape[1] * lax.axis_size("tm")
    own = by_bins(whitened)
    flipped = by_bins(jnp.stack((whitened[1], -whitened[0])))
    moving = own
    pieces = []
    for k in range(OFFSETS):
        if k == 0:
            other = own
        else:
            moving = passed_along(moving, "sta", -1)
            other = moving
        pieces.append(cross_block(own, flipped, other, windows))
    stacked = jnp.stack(pieces, axis=1)
    return lax.psum_scatter(stacked, "tm", scatter_dimension=3, tiled=True)


def kernel(count, chunks, spectra, valid, out, own, oth, ysend, yrecv, ssend, orecv):
    wins, stats, bins = spectra.shape[1:]
    half = stats // 2
    step = wins // chunks
    n = lax.axis_index("sta")
    t = lax.axis_index("tm")
    core = lax.rem(n, 2)
    odd = lax.rem(lax.div(n, 2), 2)
    inverse = 1.0 / (wins * 2)

    def around(by):
        return lax.rem(n + (by + count), count)

    barrier = pltpu.get_barrier_semaphore()
    pl.semaphore_signal(barrier, inc=1, device_id={"tm": 1 - t}, device_id_type=pl.DeviceIdType.MESH)
    for by in (-3, -2, -1, 1, 2, 3):
        pl.semaphore_signal(barrier, inc=1, device_id={"sta": around(by)}, device_id_type=pl.DeviceIdType.MESH)

    def span(j):
        return pl.ds(j * step, step)

    def y_copy(flow, j):
        h = 1 - t if flow == 0 else t
        return pltpu.make_async_remote_copy(
            src_ref=own.at[h, 0, :, span(j)], dst_ref=own.at[h, 1, :, span(j)],
            send_sem=ysend.at[flow, j], recv_sem=yrecv.at[flow, j],
            device_id={"tm": 1 - t}, device_id_type=pl.DeviceIdType.MESH)

    def y_wait(flow, j):
        h = t if flow == 0 else 1 - t
        pltpu.make_async_remote_copy(
            src_ref=own.at[h, 0, :, span(j)], dst_ref=own.at[h, 1, :, span(j)],
            send_sem=ysend.at[flow, j], recv_sem=yrecv.at[flow, j],
            device_id={"tm": 1 - t}, device_id_type=pl.DeviceIdType.MESH).wait_recv()

    def s_copy(flow, src, dst_k, s, j, dest):
        i = s * chunks + j
        return pltpu.make_async_remote_copy(
            src_ref=src, dst_ref=oth.at[dst_k, s, :, span(j)],
            send_sem=ssend.at[flow, i], recv_sem=orecv.at[dst_k, i],
            device_id={"sta": dest}, device_id_type=pl.DeviceIdType.MESH)

    near = around(1 - 2 * core)

    def direct_a(s, j):
        return s_copy(0, own.at[t, s, :, span(j)], 2 - 2 * core, s, j, around(2 * core - 3))

    def direct_b(s, j):
        return s_copy(1, own.at[t, s, :, span(j)], 1, s, j, around(-2))

    def relay_two(s, j):
        return s_copy(2, oth.at[1, s, :, span(j)], 2 * core, s, j, near)

    def relay_three(s, j):
        return s_copy(3, oth.at[2, s, :, span(j)], 1, s, j, around(1))

    sends_b = jnp.logical_or(core == 1, odd == 1)
    relays_three = jnp.logical_and(core == 1, odd == 0)
    late_two = jnp.logical_and(core == 0, odd == 1)

    def o_wait(k, s, j):
        s_copy(0, oth.at[k, s, :, span(j)], k, s, j, near).wait_recv()

    def direct(s, j):
        direct_a(s, j).start()

        @pl.when(sends_b)
        def _():
            direct_b(s, j).start()

    same = lax.broadcasted_iota(jnp.int32, (stats, stats), 0) == lax.broadcasted_iota(jnp.int32, (stats, stats), 1)

    def whiten(w, carry):
        re, im = spectra[0, w], spectra[1, w]
        power = jnp.mean(re * re + im * im, axis=-1, keepdims=True)
        row = valid[pl.ds(w, 1), :].astype(jnp.float32)
        column = jnp.sum(jnp.where(same, row, 0.0), axis=-1, keepdims=True)
        scale = column / jnp.sqrt(power + 1e-06)
        for c, part in enumerate((re, im)):
            part = part * scale
            for h in range(2):
                own[h, 0, c, w] = part[h * half:(h + 1) * half]
        return carry

    lax.fori_loop(0, step, whiten, 0, unroll=2)
    pl.semaphore_wait(barrier, 7)

    def first(j, carry):
        @pl.when(j + 1 < chunks)
        def _():
            lax.fori_loop((j + 1) * step, (j + 2) * step, whiten, 0)
        y_copy(0, j).start()
        direct(0, j)
        return carry

    lax.fori_loop(0, chunks, first, 0)

    def second(j, carry):
        y_copy(1, j).start()
        return carry

    lax.fori_loop(0, chunks, second, 0)

    def clear(r, carry):
        out[0, :, r] = jnp.zeros_like(out[0, :, r])
        out[1, :, r] = jnp.zeros_like(out[1, :, r])
        return carry

    lax.fori_loop(0, stats, clear, 0)

    def unit(other, k, s, j):
        last = jnp.logical_and(s == 1, j == chunks - 1)
        factor = jnp.where(last, inverse, 1.0)

        def block(p, carry):
            h = lax.div(p, bins // LANES)
            lanes = pl.ds(pl.multiple_of(lax.rem(p, bins // LANES) * LANES, LANES), LANES)
            for r0 in range(0, half, ROWS):
                a0 = h * half + r0
                total = [[out[ri, k, a0 + r, :, lanes] for ri in range(2)] for r in range(ROWS)]
                for v in range(step):
                    w = j * step + v
                    pr, pi = other(0, w, lanes), other(1, w, lanes)
                    for r in range(ROWS):
                        re = own[h, s, 0, w, r0 + r:r0 + r + 1, lanes]
                        im = own[h, s, 1, w, r0 + r:r0 + r + 1, lanes]
                        total[r][0] = total[r][0] + re * pr + im * pi
                        total[r][1] = total[r][1] + im * pr - re * pi
                for r in range(ROWS):
                    for ri in range(2):
                        out[ri, k, a0 + r, :, lanes] = total[r][ri] * factor
            return carry

        lax.fori_loop(0, 2 * (bins // LANES), block, 0)

    def zero_unit(s, j):
        unit(lambda c, w, lanes: own[t, s, c, w, :, lanes], 0, s, j)

    def other_units(s, j):
        def each(k, carry):
            unit(lambda c, w, lanes: oth[k, s, c, w, :, lanes], k + 1, s, j)
            return carry
        lax.fori_loop(0, OFFSETS - 1, each, 0)

    def zero_first(j, carry):
        zero_unit(0, j)
        return carry

    lax.fori_loop(0, chunks, zero_first, 0)

    def pulse(i, carry):
        @pl.when(i < chunks)
        def _():
            y_wait(0, i)
            direct(1, i)

        @pl.when(i < 2 * chunks)
        def _():
            s, j = lax.div(i, chunks), lax.rem(i, chunks)

            @pl.when(core == 1)
            def _():
                o_wait(2, s, j)

            @pl.when(relays_three)
            def _():
                relay_three(s, j).start()

            @pl.when(jnp.logical_not(late_two))
            def _():
                o_wait(1, s, j)
                relay_two(s, j).start()

        @pl.when(i >= 1)
        def _():
            s, j = lax.div(i - 1, chunks), lax.rem(i - 1, chunks)

            @pl.when(late_two)
            def _():
                o_wait(1, s, j)
                relay_two(s, j).start()

            @pl.when(s == 1)
            def _():
                y_wait(1, j)
                zero_unit(s, j)

            o_wait(0, s, j)

            @pl.when(core == 0)
            def _():
                o_wait(2, s, j)

            other_units(s, j)
        return carry

    lax.fori_loop(0, 2 * chunks + 1, pulse, 0)

    def drain(i, carry):
        s, j = lax.div(i, chunks), lax.rem(i, chunks)
        direct_a(s, j).wait_send()
        relay_two(s, j).wait_send()

        @pl.when(sends_b)
        def _():
            direct_b(s, j).wait_send()

        @pl.when(relays_three)
        def _():
            relay_three(s, j).wait_send()

        @pl.when(s == 0)
        def _():
            y_copy(0, j).wait_send()
            y_copy(1, j).wait_send()
        return carry

    lax.fori_loop(0, 2 * chunks, drain, 0)


def on_device(count, chunks, spectra, valid):
    wins, stats, bins = spectra.shape[1:]
    half = stats // 2
    return pl.pallas_call(
        functools.partial(kernel, count, chunks),
        out_shape=jax.ShapeDtypeStruct((2, OFFSETS, stats, half, bins), jnp.float32),
        in_specs=[pl.BlockSpec(memory_space=pltpu.VMEM)] * 2,
        out_specs=pl.BlockSpec(memory_space=pltpu.VMEM),
        scratch_shapes=[
            pltpu.VMEM((2, 2, 2, wins, half, bins), jnp.float32),
            pltpu.VMEM((OFFSETS - 1, 2, 2, wins, half, bins), jnp.float32),
            pltpu.SemaphoreType.DMA((2, chunks)),
            pltpu.SemaphoreType.DMA((2, chunks)),
            pltpu.SemaphoreType.DMA((4, 2 * chunks)),
            pltpu.SemaphoreType.DMA((OFFSETS - 1, 2 * chunks)),
        ],
        compiler_params=pltpu.CompilerParams(collective_id=0, has_side_effects=True),
        name="cross_stacks",
    )(spectra, valid)


def solution(mesh):
    count, slots = mesh.shape["sta"], mesh.shape["tm"]
    in_specs = (P(None, "tm", "sta", None), P("tm", "sta"))
    out_specs = P(None, None, "sta", "tm", None)

    def body(spectra, valid):
        wins, stats, bins = spectra.shape[1:]
        fits = slots == 2 and count % 4 == 0 and count >= 8
        fits = fits and wins % 8 == 0 and stats % 16 == 0 and bins % LANES == 0
        if not fits:
            return on_device_general(spectra, valid)
        return on_device(count, wins // 8, spectra, valid)

    return jax.shard_map(body, mesh=mesh, in_specs=in_specs, out_specs=out_specs, check_vma=False)
```

profile of v0, /device:TPU:3, one launch (start us, length us, event | category | flops | bytes accessed | tf_op | source)
XLA Modules:
  0.0 72.8 jit_solution(17826295381826547285)
XLA Ops:
  0.0 68.2 %cross_stacks.1 = f32[2,4,32,16,256]{4,3,2,1,0:T(8,128)} custom-call(f32[2,32,32,256]{3,2,1,0:T(8,128)} %spectra.1, s32[32,32]{1,0:T(8,128)} %valid.1), custom_call_target="tpu_custom_call" | custom-call | tf_op jit(solution)/shard_map/cross_stacks/pallas_call | solution.py:280
  68.2 4.6 %copy.4 = f32[2,4,32,16,256]{4,3,2,1,0:T(8,128)} copy(f32[2,4,32,16,256]{4,3,2,1,0:T(8,128)} %cross_stacks.1) | data formatting | bytes 8388608
where the time goes:
time: 73 us; the launch traced here: 72.8 us
  Pallas kernels  68.2 us (93%)
  local copies, waits for them, and re-layouts  4.64 us (6%)
    pallas_call x1, Pallas kernels, on_device(): pl.pallas_call(functools.partial(kernel, count, chunks), out_shape=jax.Sh...  68.2 us
    unnamed x1, local copies, waits for them, and re-layouts  4.64 us

commit v1 on v0

--- a/solution.py
+++ b/solution.py
@@ -54,7 +54,7 @@
     return lax.psum_scatter(stacked, "tm", scatter_dimension=3, tiled=True)
 
 
-def kernel(count, chunks, spectra, valid, out, own, oth, ysend, yrecv, ssend, orecv):
+def kernel(count, chunks, spectra, valid, out, raw, own, oth, lsem, osem, ysend, yrecv, ssend, orecv):
     wins, stats, bins = spectra.shape[1:]
     half = stats // 2
     step = wins // chunks
@@ -126,25 +126,35 @@
 
     same = lax.broadcasted_iota(jnp.int32, (stats, stats), 0) == lax.broadcasted_iota(jnp.int32, (stats, stats), 1)
 
-    def whiten(w, carry):
-        re, im = spectra[0, w], spectra[1, w]
-        power = jnp.mean(re * re + im * im, axis=-1, keepdims=True)
-        row = valid[pl.ds(w, 1), :].astype(jnp.float32)
-        column = jnp.sum(jnp.where(same, row, 0.0), axis=-1, keepdims=True)
-        scale = column / jnp.sqrt(power + 1e-06)
-        for c, part in enumerate((re, im)):
-            part = part * scale
-            for h in range(2):
-                own[h, 0, c, w] = part[h * half:(h + 1) * half]
-        return carry
-
-    lax.fori_loop(0, step, whiten, 0, unroll=2)
+    def load(j):
+        return pltpu.make_async_copy(spectra.at[:, span(j)], raw.at[:, span(j)], lsem.at[j])
+
+    def whiten(j):
+        load(j).wait()
+        for v in range(step):
+            w = j * step + v
+            re, im = raw[0, w], raw[1, w]
+            power = jnp.mean(re * re + im * im, axis=-1, keepdims=True)
+            row = valid[pl.ds(w, 1), :].astype(jnp.float32)
+            column = jnp.sum(jnp.where(same, row, 0.0), axis=-1, keepdims=True)
+            scale = column / jnp.sqrt(power + 1e-06)
+            for c, part in enumerate((re, im)):
+                part = part * scale
+                for h in range(2):
+                    own[h, 0, c, w] = part[h * half:(h + 1) * half]
+
+    def fetch(j, carry):
+        load(j).start()
+        return carry
+
+    lax.fori_loop(0, chunks, fetch, 0)
+    whiten(0)
     pl.semaphore_wait(barrier, 7)
 
     def first(j, carry):
         @pl.when(j + 1 < chunks)
         def _():
-            lax.fori_loop((j + 1) * step, (j + 2) * step, whiten, 0)
+            whiten(j + 1)
         y_copy(0, j).start()
         direct(0, j)
         return carry
@@ -189,12 +199,21 @@
 
         lax.fori_loop(0, 2 * (bins // LANES), block, 0)
 
+    def leave(k):
+        return pltpu.make_async_copy(out.at[:, k], result.at[:, k], osem.at[k])
+
+    def emit(k, s, j):
+        @pl.when(jnp.logical_and(s == 1, j == chunks - 1))
+        def _():
+            pass
+
     def zero_unit(s, j):
         unit(lambda c, w, lanes: own[t, s, c, w, :, lanes], 0, s, j)
 
     def other_units(s, j):
         def each(k, carry):
             unit(lambda c, w, lanes: oth[k, s, c, w, :, lanes], k + 1, s, j)
+            emit(k + 1, s, j)
             return carry
         lax.fori_loop(0, OFFSETS - 1, each, 0)
 
@@ -240,6 +259,7 @@
             def _():
                 y_wait(1, j)
                 zero_unit(s, j)
+                emit(0, s, j)
 
             o_wait(0, s, j)
 
@@ -272,6 +292,9 @@
         return carry
 
     lax.fori_loop(0, 2 * chunks, drain, 0)
+
+    for k in range(OFFSETS):
+        pass
 
 
 def on_device(count, chunks, spectra, valid):
@@ -280,17 +303,21 @@
     return pl.pallas_call(
         functools.partial(kernel, count, chunks),
         out_shape=jax.ShapeDtypeStruct((2, OFFSETS, stats, half, bins), jnp.float32),
-        in_specs=[pl.BlockSpec(memory_space=pltpu.VMEM)] * 2,
+        in_specs=[pl.BlockSpec(memory_space=pltpu.HBM), pl.BlockSpec(memory_space=pltpu.VMEM)],
         out_specs=pl.BlockSpec(memory_space=pltpu.VMEM),
         scratch_shapes=[
+            pltpu.VMEM((2, wins, stats, bins), jnp.float32),
             pltpu.VMEM((2, 2, 2, wins, half, bins), jnp.float32),
             pltpu.VMEM((OFFSETS - 1, 2, 2, wins, half, bins), jnp.float32),
+            pltpu.SemaphoreType.DMA((chunks,)),
+            pltpu.SemaphoreType.DMA((OFFSETS,)),
             pltpu.SemaphoreType.DMA((2, chunks)),
             pltpu.SemaphoreType.DMA((2, chunks)),
             pltpu.SemaphoreType.DMA((4, 2 * chunks)),
             pltpu.SemaphoreType.DMA((OFFSETS - 1, 2 * chunks)),
         ],
-        compiler_params=pltpu.CompilerParams(collective_id=0, has_side_effects=True),
+        compiler_params=pltpu.CompilerParams(
+            collective_id=0, has_side_effects=True, vmem_limit_bytes=24 * 1024 * 1024),
         name="cross_stacks",
     )(spectra, valid)
 
@@ -306,6 +333,6 @@
         fits = fits and wins % 8 == 0 and stats % 16 == 0 and bins % LANES == 0
         if not fits:
             return on_device_general(spectra, valid)
-        return on_device(count, wins // 8, spectra, valid)
+        return on_device(count, wins // 4, spectra, valid)
 
     return jax.shard_map(body, mesh=mesh, in_specs=in_specs, out_specs=out_specs, check_vma=False)

time: 73 us -> 66.3 us (0.908)
  Pallas kernels: 68.2 us -> 61.8 us
    pallas_call x1, Pallas kernels: 68.2 us -> 61.8 us  [on_device(): pl.pallas_call(functools.partial(kernel, count, chunks), out_shape=jax.Sh...]
    unnamed x1 -> x5, local copies, waits for them, and re-layouts: 4.64 us -> 4.32 us
where the time goes in v1:
time: 66.3 us; the launch traced here: 66.1 us
  Pallas kernels  61.8 us (93%)
  local copies, waits for them, and re-layouts  4.32 us (7%)
    pallas_call x1, Pallas kernels, on_device(): pl.pallas_call(functools.partial(kernel, count, chunks), out_shape=jax.Sh...  61.8 us
    unnamed x5, local copies, waits for them, and re-layouts  4.32 us

profile of v1, /device:TPU:3, one launch (start us, length us, event | category | flops | bytes accessed | tf_op | source)
XLA Modules:
  0.0 66.1 jit_solution(881080818075239591)
XLA Ops:
  0.0 0.0 copy-start
  0.0 1.6 %copy-done = f32[2,32,32,256]{3,2,1,0:T(8,128)S(1)} copy-done((f32[2,32,32,256]{3,2,1,0:T(8,128)S(1)}, f32[2,32,32,256]{3,2,1,0:T(8,128)}, u32[]{:S(2)}) %copy-start) | copy-done | bytes 2097176
  1.6 0.0 copy-start.1
  1.6 0.7 %copy-done.1 = s32[32,32]{1,0:T(8,128)S(1)} copy-done((s32[32,32]{1,0:T(8,128)S(1)}, s32[32,32]{1,0:T(8,128)}, u32[]{:S(2)}) %copy-start.1) | copy-done | bytes 4120
  2.3 61.8 %cross_stacks.1 = f32[2,4,32,16,256]{4,3,2,1,0:T(8,128)S(1)} custom-call(f32[2,32,32,256]{3,2,1,0:T(8,128)S(1)} %copy-done, s32[32,32]{1,0:T(8,128)S(1)} %copy-done.1), custom_call_target="tpu_custom_call" | custom-call | tf_op jit(solution)/shard_map/cross_stacks/pallas_call | solution.py:303
  64.1 2.0 %copy.4 = f32[2,4,32,16,256]{4,3,2,1,0:T(8,128)} copy(f32[2,4,32,16,256]{4,3,2,1,0:T(8,128)S(1)} %cross_stacks.1) | data formatting | bytes 8388608
Async XLA Ops:
  0.0 1.6 %copy-start = (f32[2,32,32,256]{3,2,1,0:T(8,128)S(1)}, f32[2,32,32,256]{3,2,1,0:T(8,128)}, u32[]{:S(2)}) copy-start(f32[2,32,32,256]{3,2,1,0:T(8,128)} %spectra.1) | copy-start | bytes 6291460
  1.6 0.7 %copy-start.1 = (s32[32,32]{1,0:T(8,128)S(1)}, s32[32,32]{1,0:T(8,128)}, u32[]{:S(2)}) copy-start(s32[32,32]{1,0:T(8,128)} %valid.1) | copy-start | bytes 12292

commit v2 on v1

--- a/solution.py
+++ b/solution.py
@@ -54,7 +54,7 @@
     return lax.psum_scatter(stacked, "tm", scatter_dimension=3, tiled=True)
 
 
-def kernel(count, chunks, spectra, valid, out, raw, own, oth, lsem, osem, ysend, yrecv, ssend, orecv):
+def kernel(count, chunks, spectra, valid, out, raw, own, oth, lsem, ysend, yrecv, ssend, orecv):
     wins, stats, bins = spectra.shape[1:]
     half = stats // 2
     step = wins // chunks
@@ -183,38 +183,39 @@
             lanes = pl.ds(pl.multiple_of(lax.rem(p, bins // LANES) * LANES, LANES), LANES)
             for r0 in range(0, half, ROWS):
                 a0 = h * half + r0
-                total = [[out[ri, k, a0 + r, :, lanes] for ri in range(2)] for r in range(ROWS)]
+                total = [None] * ROWS
                 for v in range(step):
                     w = j * step + v
                     pr, pi = other(0, w, lanes), other(1, w, lanes)
+                    pd = pr - pi
                     for r in range(ROWS):
                         re = own[h, s, 0, w, r0 + r:r0 + r + 1, lanes]
                         im = own[h, s, 1, w, r0 + r:r0 + r + 1, lanes]
-                        total[r][0] = total[r][0] + re * pr + im * pi
-                        total[r][1] = total[r][1] + im * pr - re * pi
+                        terms = (re * pr, im * pi, (re + im) * pd)
+                        total[r] = terms if v == 0 else tuple(x + y for x, y in zip(total[r], terms))
                 for r in range(ROWS):
+                    first_term, second_term, third_term = total[r]
+                    pair = (first_term + second_term, third_term - first_term + second_term)
                     for ri in range(2):
-                        out[ri, k, a0 + r, :, lanes] = total[r][ri] * factor
+                        out[ri, k, a0 + r, :, lanes] = (out[ri, k, a0 + r, :, lanes] + pair[ri]) * factor
             return carry
 
         lax.fori_loop(0, 2 * (bins // LANES), block, 0)
-
-    def leave(k):
-        return pltpu.make_async_copy(out.at[:, k], result.at[:, k], osem.at[k])
-
-    def emit(k, s, j):
-        @pl.when(jnp.logical_and(s == 1, j == chunks - 1))
-        def _():
-            pass
 
     def zero_unit(s, j):
         unit(lambda c, w, lanes: own[t, s, c, w, :, lanes], 0, s, j)
 
     def other_units(s, j):
-        def each(k, carry):
+        def each(p, carry):
+            k = jnp.where(p == 0, 1, jnp.where(p == 1, 2 * core, 2 - 2 * core))
+
+            @pl.when(jnp.logical_or(p == 2, jnp.logical_and(p == 1, core == 0)))
+            def _():
+                o_wait(k, s, j)
+
             unit(lambda c, w, lanes: oth[k, s, c, w, :, lanes], k + 1, s, j)
-            emit(k + 1, s, j)
             return carry
+
         lax.fori_loop(0, OFFSETS - 1, each, 0)
 
     def zero_first(j, carry):
@@ -259,13 +260,6 @@
             def _():
                 y_wait(1, j)
                 zero_unit(s, j)
-                emit(0, s, j)
-
-            o_wait(0, s, j)
-
-            @pl.when(core == 0)
-            def _():
-                o_wait(2, s, j)
 
             other_units(s, j)
         return carry
@@ -292,9 +286,6 @@
         return carry
 
     lax.fori_loop(0, 2 * chunks, drain, 0)
-
-    for k in range(OFFSETS):
-        pass
 
 
 def on_device(count, chunks, spectra, valid):
@@ -310,7 +301,6 @@
             pltpu.VMEM((2, 2, 2, wins, half, bins), jnp.float32),
             pltpu.VMEM((OFFSETS - 1, 2, 2, wins, half, bins), jnp.float32),
             pltpu.SemaphoreType.DMA((chunks,)),
-            pltpu.SemaphoreType.DMA((OFFSETS,)),
             pltpu.SemaphoreType.DMA((2, chunks)),
             pltpu.SemaphoreType.DMA((2, chunks)),
             pltpu.SemaphoreType.DMA((4, 2 * chunks)),

time: 66.3 us -> 64.2 us (0.968)
  Pallas kernels: 61.8 us -> 59.4 us
    pallas_call x1, Pallas kernels: 61.8 us -> 59.4 us  [on_device(): pl.pallas_call(functools.partial(kernel, count, chunks), out_shape=jax.Sh...]
where the time goes in v2:
time: 64.2 us; the launch traced here: 63.7 us
  Pallas kernels  59.4 us (93%)
  local copies, waits for them, and re-layouts  4.32 us (7%)
    pallas_call x1, Pallas kernels, on_device(): pl.pallas_call(functools.partial(kernel, count, chunks), out_shape=jax.Sh...  59.4 us
    unnamed x5, local copies, waits for them, and re-layouts  4.32 us

profile of v2, /device:TPU:3, one launch (start us, length us, event | category | flops | bytes accessed | tf_op | source)
XLA Modules:
  0.0 63.7 jit_solution(5958491117479091321)
XLA Ops:
  0.0 0.0 copy-start
  0.0 1.6 %copy-done = f32[2,32,32,256]{3,2,1,0:T(8,128)S(1)} copy-done((f32[2,32,32,256]{3,2,1,0:T(8,128)S(1)}, f32[2,32,32,256]{3,2,1,0:T(8,128)}, u32[]{:S(2)}) %copy-start) | copy-done | bytes 2097176
  1.6 0.0 copy-start.1
  1.6 0.7 %copy-done.1 = s32[32,32]{1,0:T(8,128)S(1)} copy-done((s32[32,32]{1,0:T(8,128)S(1)}, s32[32,32]{1,0:T(8,128)}, u32[]{:S(2)}) %copy-start.1) | copy-done | bytes 4120
  2.3 59.4 %cross_stacks.1 = f32[2,4,32,16,256]{4,3,2,1,0:T(8,128)S(1)} custom-call(f32[2,32,32,256]{3,2,1,0:T(8,128)S(1)} %copy-done, s32[32,32]{1,0:T(8,128)S(1)} %copy-done.1), custom_call_target="tpu_custom_call" | custom-call | tf_op jit(solution)/shard_map/cross_stacks/pallas_call | solution.py:294
  61.7 2.0 %copy.4 = f32[2,4,32,16,256]{4,3,2,1,0:T(8,128)} copy(f32[2,4,32,16,256]{4,3,2,1,0:T(8,128)S(1)} %cross_stacks.1) | data formatting | bytes 8388608
Async XLA Ops:
  0.0 1.6 %copy-start = (f32[2,32,32,256]{3,2,1,0:T(8,128)S(1)}, f32[2,32,32,256]{3,2,1,0:T(8,128)}, u32[]{:S(2)}) copy-start(f32[2,32,32,256]{3,2,1,0:T(8,128)} %spectra.1) | copy-start | bytes 6291460
  1.6 0.7 %copy-start.1 = (s32[32,32]{1,0:T(8,128)S(1)}, s32[32,32]{1,0:T(8,128)}, u32[]{:S(2)}) copy-start(s32[32,32]{1,0:T(8,128)} %valid.1) | copy-start | bytes 12292
